TPU v7x, 128 devices: a whole 4x4x4 slice. The times are simulated.
128 devices in a mesh: row: 16 (over x, z), col: 8 (over y, core).
Axes of the slice: x: 4, y: 4, z: 4, core: 2. Of those that a mesh axis runs over, the one named last changes fastest.
Arguments:
- posteriors: bfloat16 [8192, 256, 256], P(('row', 'col'))
- pair_anchor: int32 [8192], P(('row', 'col')), may hold values from 0 to 15, as said below
- pair_column: int32 [8192], P(('row', 'col')), may hold values from 0 to 511
- inter: int32 [32, 4], replicated, may hold values from 0 to 15, all different within a row
- lengths: int32 [512], replicated, may hold values from 32 to 256
Outputs:
- consistent: bfloat16 [32, 512, 256, 256], P(None, ('row', 'col'))
Inputs may be any that keep to these rules, and one draw needn't show every extreme that they name: `pair_anchor`: each anchor and family sequence pair (a, y) stands in exactly one slot over all devices. The slots of one device hold at most 1 pairs whose columns lie in one aligned block of 4 columns, and every device reaches that bound for some block. `inter`: the 4 anchors of a row differ.
All inputs are finite; a program needn't handle non-finite values.
Results may differ from a plain program's by a relative error of at most 0.001.
Values may be sent and summed in bfloat16 or wider, within the bound.
No kernel may reach another device: no remote copies, remote signals or barrier semaphores. Data moves between devices by JAX's collectives and lax.ppermute only.
A program may use at most 384 MiB of HBM per device.

v0:
```python
import jax
import jax.numpy as jnp
from jax import lax
from jax.sharding import PartitionSpec as P

NZ = 16
INTER = 4
YB = 4


def broadcast(block, axis, source):
    block = jnp.where(lax.axis_index(axis) == source, block, jnp.zeros_like(block))
    return lax.psum(block, axis)


def shards(posteriors, pair_anchor, pair_column, inter, lengths):
    devices = lax.axis_size(("row", "col"))
    my_index = lax.axis_index(("row", "col"))
    slot_count = posteriors.shape[0]
    side_len = posteriors.shape[1]
    col_block = YB
    capacity = max(1, 2 * slot_count // devices)
    target = pair_column // col_block
    slot_order = jnp.arange(slot_count, dtype=jnp.int32)
    earlier = (target[:, None] == target[None, :]) & (slot_order[None, :] < slot_order[:, None])
    slot_rank = jnp.sum(earlier.astype(jnp.int32), axis=1)
    where_to = target * capacity + slot_rank
    slot_keys = pair_anchor * col_block + pair_column % col_block
    outgoing = (
        jnp.zeros((devices * capacity, side_len, side_len), jnp.bfloat16)
        .at[where_to]
        .set(posteriors)
    )
    out_keys = (
        jnp.full((devices * capacity,), NZ * col_block, jnp.int32).at[where_to].set(slot_keys)
    )
    incoming, in_keys = (
        lax.all_to_all(outgoing, ("row", "col"), split_axis=0, concat_axis=0, tiled=True),
        lax.all_to_all(out_keys, ("row", "col"), split_axis=0, concat_axis=0, tiled=True),
    )
    slab = (
        jnp.zeros((NZ * col_block, side_len, side_len), jnp.bfloat16)
        .at[in_keys]
        .set(incoming, mode="drop")
    )
    slab = slab.reshape(NZ, col_block, side_len, side_len)
    own_rows = lax.dynamic_slice_in_dim(inter, my_index * col_block, col_block, 0)
    local_cols = jnp.arange(col_block, dtype=jnp.int32)[:, None]
    own_window = slab[own_rows, local_cols]
    pieces = [broadcast(own_window, ("row", "col"), owner) for owner in range(lax.axis_size("col"))]
    window = jnp.concatenate(pieces, axis=0)
    window_rows = window.shape[0]
    summed = jnp.zeros((window_rows, col_block, side_len, side_len), jnp.float32)
    for term in range(INTER):
        left_side = window[:, term]
        right_side = slab[inter[:, term]]
        summed = summed + jnp.einsum(
            "xmi,xymj->xyij", left_side, right_side, preferred_element_type=jnp.float32
        )
    position = jnp.arange(side_len, dtype=jnp.int32)
    row_lengths = lengths[:window_rows]
    col_lengths = lax.dynamic_slice_in_dim(lengths, my_index * col_block, col_block, 0)
    row_mask = (position[None, :] < row_lengths[:, None]).astype(jnp.float32)
    col_mask = (position[None, :] < col_lengths[:, None]).astype(jnp.float32)
    scaled = summed * (1.0 / INTER) * row_mask[:, None, :, None] * col_mask[None, :, None, :]
    return scaled.astype(jnp.bfloat16)


def solution(mesh):
    return jax.shard_map(
        shards,
        mesh=mesh,
        in_specs=(P(("row", "col"), None, None), P(("row", "col")), P(("row", "col")), P(), P()),
        out_specs=P(None, ("row", "col"), None, None),
        check_vma=False,
    )
```

profile of v0, /device:TPU:1, one launch (start us, length us, event | category | flops | bytes accessed | tf_op | source)
XLA Modules:
  0.0 727.6 jit_solution(17250908003385226376)
XLA Ops:
  6.5 0.7 fusion.9
  7.2 0.2 convert_reduce_fusion
  7.4 0.8 scatter_custom_fusion
  8.2 0.7 copy.52
  8.9 11.5 %all-to-all-start = ((s32[128,1,1]{2,1,0:T(1,128)}), s32[128,1,1]{2,1,0:T(1,128)S(1)}, u32[]{:S(2)}, u32[]{:S(2)}) async-start(s32[128,1,1]{2,1,0:T(1,128)} %copy.52), calls=%async_computation | async-start | bytes 131072 | tf_op jit(solution)/shard_map/all_to_all | solution.py:39
  20.4 6.1 broadcast_in_dim.12
  26.5 21.9 %scatter_fusion = bf16[128,256,256]{2,1,0:T(8,128)(2,1)} fusion(bf16[128,256,256]{2,1,0:T(8,128)(2,1)} %broadcast_in_dim.12, s32[64]{0:T(128)S(1)} %compare_select_fusion.6, bf16[64,256,256]{2,1,0:T(8,128)(2,1)} %param.5), kind=kCustom, calls=%fused_computation.6 | custom fusion | bytes 25166080 | tf_op jit(solution)/shard_map/scatter | solution.py:32
  48.4 0.0 copy-start.4
  48.4 0.0 all-to-all-done
  48.4 10.2 %all-to-all-start.1 = ((bf16[128,256,256]{2,1,0:T(8,128)(2,1)}), bf16[128,256,256]{2,1,0:T(8,128)(2,1)}, u32[]{:S(2)}, u32[]{:S(2)}) async-start(bf16[128,256,256]{2,1,0:T(8,128)(2,1)} %scatter_fusion), calls=%async_computation.1 | async-start | bytes 33554432 | tf_op jit(solution)/shard_map/all_to_all | solution.py:38
  58.6 0.0 all-reduce.3.cloned.1.call-start
  58.7 0.0 copy-done.4
  58.7 0.1 fusion.8
  58.8 0.1 copy.53
  58.9 0.1 reshape.86
  59.0 2.4 reduce
  61.3 224.9 %all-to-all-done.1 = bf16[128,256,256]{2,1,0:T(8,128)(2,1)} async-done(((bf16[128,256,256]{2,1,0:T(8,128)(2,1)}), bf16[128,256,256]{2,1,0:T(8,128)(2,1)}, u32[]{:S(2)}, u32[]{:S(2)}) %all-to-all-start.1) | async-done | bytes 16777248 | tf_op jit(solution)/shard_map/all_to_all | solution.py:38
  286.2 4.2 broadcast_in_dim.10
  290.5 41.8 %scatter_fusion.1 = bf16[64,256,256]{2,1,0:T(8,128)(2,1)} fusion(bf16[64,256,256]{2,1,0:T(8,128)(2,1)} %broadcast_in_dim.10, s32[128]{0:T(128)S(1)} %fusion.10, bf16[128,256,256]{2,1,0:T(8,128)(2,1)} %all-to-all-done.1), kind=kCustom, calls=%fused_computation.7 | custom fusion | bytes 50332160 | tf_op jit(solution)/shard_map/scatter | solution.py:44
  332.3 4.1 gather_fusion.1
  336.4 1.1 broadcast_select_fusion
  337.5 1.5 copy.61
  339.1 1.5 copy.60
  340.5 1.6 copy.59
  342.1 1.5 copy.58
  343.6 0.0 copy-start.5
  343.6 0.0 slice-start
  343.6 1.5 copy.57
  345.1 1.5 copy.56
  346.6 1.5 copy.55
  348.1 1.5 copy.54
  349.7 0.0 all-reduce.3.cloned.1.call-update
  349.7 0.0 copy-done.5
  349.7 0.1 dynamic_slice.7
  349.8 0.1 fusion.6
  349.9 0.0 slice-done
  349.9 0.1 fusion.5
  350.0 10.6 %gather_fusion.4 = bf16[32,4,256,256]{3,2,1,0:T(8,128)(2,1)} fusion(bf16[16,4,256,256]{3,2,1,0:T(8,128)(2,1)} %bitcast.64, s32[1024]{0:T(1024)S(1)} %get-tuple-element.27), kind=kCustom, calls=%fused_computation.4 | custom fusion | bytes 33554560 | tf_op jit(solution)/shard_map/gather | solution.py:56
  360.6 10.8 %gather_fusion.3 = bf16[32,4,256,256]{3,2,1,0:T(8,128)(2,1)} fusion(bf16[16,4,256,256]{3,2,1,0:T(8,128)(2,1)} %bitcast.65, s32[1024]{0:T(1024)S(1)} %get-tuple-element.28), kind=kCustom, calls=%fused_computation.3 | custom fusion | bytes 33554560 | tf_op jit(solution)/shard_map/gather | solution.py:56
  371.4 10.8 %gather_fusion.2 = bf16[32,4,256,256]{3,2,1,0:T(8,128)(2,1)} fusion(bf16[16,4,256,256]{3,2,1,0:T(8,128)(2,1)} %bitcast.66, s32[1024]{0:T(1024)S(1)} %get-tuple-element.29), kind=kCustom, calls=%fused_computation.2 | custom fusion | bytes 33554560 | tf_op jit(solution)/shard_map/gather | solution.py:56
  382.2 11.1 %gather_fusion = bf16[32,4,256,256]{3,2,1,0:T(8,128)(2,1)} fusion(bf16[16,4,256,256]{3,2,1,0:T(8,128)(2,1)} %bitcast.67, s32[1024]{0:T(1024)S(1)} %get-tuple-element.30), kind=kCustom, calls=%fused_computation | custom fusion | bytes 33554560 | tf_op jit(solution)/shard_map/gather | solution.py:56
  393.4 185.1 %all-reduce.3.cloned.1.call-done = (bf16[4,4,256,256]{3,2,0,1:T(8,128)(2,1)}, bf16[4,4,256,256]{3,2,0,1:T(8,128)(2,1)}, bf16[4,4,256,256]{3,2,0,1:T(8,128)(2,1)}...) async-done(((bf16[4,4,256,256]{3,2,0,1:T(8,128)(2,1)}, ...) | async-done | bytes 16777232 | tf_op jit(solution)/shard_map/psum | solution.py:13
  578.5 0.0 copy-start.3
  578.5 0.0 copy-start.2
  578.5 0.0 copy-start.1
  578.5 0.0 copy-start
  578.5 3.2 constant_dynamic-update-slice_fusion.7
  581.7 3.7 constant_dynamic-update-slice_fusion.6
  585.4 3.0 constant_dynamic-update-slice_fusion.5
  588.5 3.0 constant_dynamic-update-slice_fusion.4
  591.5 0.0 copy-done.3
  591.5 1.4 constant_dynamic-update-slice_fusion.3
  592.9 0.0 copy-done.2
  593.0 1.4 constant_dynamic-update-slice_fusion.2
  594.4 0.0 copy-done.1
  594.4 1.4 constant_dynamic-update-slice_fusion.1
  595.8 0.0 copy-done
  595.8 1.4 constant_dynamic-update-slice_fusion
  597.2 18.9 %fusion.3 = f32[32,4,256,256]{3,2,1,0:T(8,128)} fusion(bf16[32,4,256,256]{3,2,1,0:T(8,128)(2,1)} %gather_fusion, bf16[32,4,256,256]{3,2,0,1:T(8,128)(2,1)} %constant_dynamic-update-slice_fusion), kind=kOutput, calls=%fused_computation.16 | convolution fusion | flops 4294967296 | bytes 54525952 | tf_op jit(solution)/shard_map/xmi,xymj->xyij/dot_general | solution.py:57
  616.1 18.9 %fusion.2 = f32[32,4,256,256]{3,2,1,0:T(8,128)} fusion(bf16[32,4,256,256]{3,2,1,0:T(8,128)(2,1)} %gather_fusion.2, bf16[32,4,256,256]{3,2,0,1:T(8,128)(2,1)} %constant_dynamic-update-slice_fusion), kind=kOutput, calls=%fused_computation.14 | convolution fusion | flops 4294967296 | bytes 54525952 | tf_op jit(solution)/shard_map/xmi,xymj->xyij/dot_general | solution.py:57
  635.0 18.9 %fusion.1 = f32[32,4,256,256]{3,2,1,0:T(8,128)} fusion(bf16[32,4,256,256]{3,2,1,0:T(8,128)(2,1)} %gather_fusion.3, bf16[32,4,256,256]{3,2,0,1:T(8,128)(2,1)} %constant_dynamic-update-slice_fusion), kind=kOutput, calls=%fused_computation.12 | convolution fusion | flops 4294967296 | bytes 54525952 | tf_op jit(solution)/shard_map/xmi,xymj->xyij/dot_general | solution.py:57
  653.9 44.3 %fusion = bf16[32,4,256,256]{2,3,1,0:T(8,128)(2,1)} fusion(f32[32,4,256,256]{3,2,1,0:T(8,128)} %fusion.1, f32[32,4,256,256]{3,2,1,0:T(8,128)} %fusion.3, f32[32,4,256,256]{3,2,1,0:T(8,128)} %fusion.2, f32[4,256]{1,0:T(4,128)S(1)} %fusion.6, f32[32,256]{1,0:T(8,128)S(1)} %fusion.5, bf16[32,4,256,256]{3,2,1,0:T(8,128)(2,1)} %gather_fusion.4, ...), kind=kOutput, calls=%fused_computation.9 | convolution fusion | flops 4345298944 | bytes 138448896 | tf_op jit(solution)/shard_map/xmi,xymj->xyij/dot_general | solution.py:57
  698.3 22.5 %copy.66 = bf16[32,4,256,256]{3,2,1,0:T(8,128)(2,1)} copy(bf16[32,4,256,256]{2,3,1,0:T(8,128)(2,1)} %fusion) | data formatting | bytes 33554432 | tf_op jit(solution)/shard_map/convert_element_type | solution.py:66
  (6 shorter events, 0.0 us)
Async XLA Ops:
  8.9 39.5 %all-to-all-start = ((s32[128,1,1]{2,1,0:T(1,128)}), s32[128,1,1]{2,1,0:T(1,128)S(1)}, u32[]{:S(2)}, u32[]{:S(2)}) async-start(s32[128,1,1]{2,1,0:T(1,128)} %copy.52), calls=%async_computation | async-start | bytes 131072 | tf_op jit(solution)/shard_map/all_to_all | solution.py:39
  48.4 10.3 %copy-start.4 = (s32[32,4]{0,1:T(4,128)S(1)}, s32[32,4]{0,1:T(4,128)}, u32[]{:S(2)}) copy-start(s32[32,4]{0,1:T(4,128)} %param.8) | copy-start | bytes 1540
  48.4 237.9 %all-to-all-start.1 = ((bf16[128,256,256]{2,1,0:T(8,128)(2,1)}), bf16[128,256,256]{2,1,0:T(8,128)(2,1)}, u32[]{:S(2)}, u32[]{:S(2)}) async-start(bf16[128,256,256]{2,1,0:T(8,128)(2,1)} %scatter_fusion), calls=%async_computation.1 | async-start | bytes 33554432 | tf_op jit(solution)/shard_map/all_to_all | solution.py:38
  58.6 519.9 %all-reduce.3.cloned.1.call-start = ((), (), s32[]{:S(2)}) async-start(), calls=%async_computation.2 | async-start | bytes 33554432 | tf_op jit(solution)/shard_map/psum | solution.py:13
  343.6 6.1 copy-start.5
  343.6 6.3 slice-start
  578.5 13.0 %copy-start.3 = (bf16[4,4,256,256]{3,2,0,1:T(8,128)(2,1)S(1)}, bf16[4,4,256,256]{3,2,0,1:T(8,128)(2,1)}, u32[]{:S(2)}) copy-start(bf16[4,4,256,256]{3,2,0,1:T(8,128)(2,1)} %get-tuple-element.9) | copy-start | bytes 6291460
  578.5 14.4 %copy-start.2 = (bf16[4,4,256,256]{3,2,0,1:T(8,128)(2,1)S(1)}, bf16[4,4,256,256]{3,2,0,1:T(8,128)(2,1)}, u32[]{:S(2)}) copy-start(bf16[4,4,256,256]{3,2,0,1:T(8,128)(2,1)} %get-tuple-element.10) | copy-start | bytes 6291460
  578.5 15.9 %copy-start.1 = (bf16[4,4,256,256]{3,2,0,1:T(8,128)(2,1)S(1)}, bf16[4,4,256,256]{3,2,0,1:T(8,128)(2,1)}, u32[]{:S(2)}) copy-start(bf16[4,4,256,256]{3,2,0,1:T(8,128)(2,1)} %get-tuple-element.11) | copy-start | bytes 6291460
  578.5 17.3 %copy-start = (bf16[4,4,256,256]{3,2,0,1:T(8,128)(2,1)S(1)}, bf16[4,4,256,256]{3,2,0,1:T(8,128)(2,1)}, u32[]{:S(2)}) copy-start(bf16[4,4,256,256]{3,2,0,1:T(8,128)(2,1)} %get-tuple-element.12) | copy-start | bytes 6291460
Sparse Core Ops, SparseCore 0:
  349.8 228.6 all-reduce.2
where the time goes:
time: 730 us; the launch traced here: 728 us
  waiting for transfers between devices  410 us (56%)
  local copies, waits for them, and re-layouts  177 us (24%)
  matrix products  101 us (14%)
  starting transfers between devices  21.7 us (3%)
  between operations  13.5 us (2%)
    all_to_all x1, waiting for transfers between devices, shards(): lax.all_to_all(outgoing, ('row', 'col'), split_axis=0, concat_axis=0, til...  225 us
    psum x1, waiting for transfers between devices, broadcast(): return lax.psum(block, axis)  185 us
    dot_general x4, matrix products, shards(): jnp.einsum('xmi,xymj->xyij', left_side, right_side, preferred_element_typ...  101 us
    gather x4, local copies, waits for them, and re-layouts, shards(): right_side = slab[inter[:, term]]  43.4 us
    scatter x1, local copies, waits for them, and re-layouts, shards(): slab = jnp.zeros((NZ * col_block, side_len, side_len), jnp.bfloat16).at[i...  41.8 us
    convert_element_type x1, local copies, waits for them, and re-layouts, shards(): return scaled.astype(jnp.bfloat16)  22.5 us
    scatter x1, local copies, waits for them, and re-layouts, shards(): outgoing = jnp.zeros((devices * capacity, side_len, side_len), jnp.bfloat...  21.9 us
    unnamed x19, local copies, waits for them, and re-layouts  17.3 us
  transfers between devices with their start and end apart: 3, of which 2 were waited for; matrix products, arithmetic and copies ran while one was open for 10% of the time, Pallas kernels for 0%

commit v1 on v0

v1 whole, which is shorter than its diff:
```python
import jax
import jax.numpy as jnp
from jax import lax
from jax.experimental import pallas as pl
from jax.experimental.pallas import tpu as pltpu
from jax.sharding import PartitionSpec as P

NZ = 16
INTER = 4
YB = 4
STORES = 4
AXES = ("row", "col")
VMEM_LIMIT = 56 * 1024 * 1024
TRANSFORM_VMEM = 56 * 1024 * 1024


def pack_kernel(slot_target_ref, blocks_ref, out_ref, held_ref, load_sems, store_sem):
    chunks = load_sems.shape[0]
    slots = held_ref.shape[0]
    chunk = slots // chunks

    def load(c):
        part = pl.ds(c * chunk, chunk)
        return pltpu.make_async_copy(blocks_ref.at[part], held_ref.at[part], load_sems.at[c])

    for c in range(chunks):
        load(c).start()
    for c in range(chunks):
        load(c).wait()
        for s in range(c * chunk, (c + 1) * chunk):
            pltpu.make_async_copy(
                held_ref.at[s], out_ref.at[slot_target_ref[s]], store_sem
            ).start()
    pltpu.make_async_copy(held_ref, out_ref.at[pl.ds(0, slots)], store_sem).wait()


def pack(posteriors, slot_target, devices):
    slots, side, _ = posteriors.shape
    chunks = 8
    return pl.pallas_call(
        pack_kernel,
        out_shape=jax.ShapeDtypeStruct((devices, side, side), posteriors.dtype),
        in_specs=[
            pl.BlockSpec(memory_space=pltpu.SMEM),
            pl.BlockSpec(memory_space=pl.ANY),
        ],
        out_specs=pl.BlockSpec(memory_space=pl.ANY),
        scratch_shapes=[
            pltpu.VMEM((slots, side, side), posteriors.dtype),
            pltpu.SemaphoreType.DMA((chunks,)),
            pltpu.SemaphoreType.DMA,
        ],
        compiler_params=pltpu.CompilerParams(vmem_limit_bytes=VMEM_LIMIT),
        name="pack",
    )(slot_target, posteriors)


def pieces_kernel(owner_slot_ref, sent_key_ref, block_ref, out_ref):
    pieces, _, rows, side = out_ref.shape
    tile = side // pieces
    o = pl.program_id(0)
    owners = pl.num_programs(0)
    turned = block_ref[0].T
    out_ref[:, 0, :tile, :] = turned.reshape(pieces, tile, side)
    for p in range(pieces):
        first = lax.broadcasted_iota(jnp.int32, (rows - tile, side), 0) < (rows - tile) // 2
        keys = jnp.where(first, sent_key_ref[p * owners + o], sent_key_ref[o])
        out_ref[p, 0, tile:, :] = keys.astype(jnp.float32).astype(out_ref.dtype)


def window_pieces(posteriors, owner_slot, sent_key, pieces):
    _, side, _ = posteriors.shape
    owners = owner_slot.shape[0]
    rows = side // pieces + 8
    return pl.pallas_call(
        pieces_kernel,
        out_shape=jax.ShapeDtypeStruct((pieces, owners, rows, side), posteriors.dtype),
        grid_spec=pltpu.PrefetchScalarGridSpec(
            num_scalar_prefetch=2,
            grid=(owners,),
            in_specs=[pl.BlockSpec((1, side, side), lambda o, slot, key: (slot[o], 0, 0))],
            out_specs=pl.BlockSpec((pieces, 1, rows, side), lambda o, slot, key: (0, o, 0, 0)),
        ),
        name="pieces",
    )(owner_slot, sent_key, posteriors)


def pick_kernel(wanted_ref, arrived_ref, picked_ref, source_ref, found_ref, where_ref, sem):
    wanted, tile, side = picked_ref.shape
    devices = arrived_ref.shape[0]
    keys = lax.broadcasted_iota(jnp.int32, (devices, side), 1)
    device = lax.broadcasted_iota(jnp.int32, (devices, side), 0)
    for part in range(2):
        got = arrived_ref[:, tile + 4 * part, :].astype(jnp.float32).astype(jnp.int32)
        found = jnp.sum(jnp.where(got == keys, device, 0), axis=0, keepdims=True)
        found_ref[pl.ds(part, 1), :] = found
    source_ref[...] = found_ref[pl.ds(0, 1), :]
    copy = pltpu.make_async_copy(found_ref, where_ref, sem)
    copy.start()
    copy.wait()
    for q in range(wanted):
        picked_ref[q] = arrived_ref[where_ref[1, wanted_ref[q]], :tile, :]


def pick(arrived, wanted, tile):
    devices, _, side = arrived.shape
    count = wanted.shape[0]
    return pl.pallas_call(
        pick_kernel,
        out_shape=(
            jax.ShapeDtypeStruct((count, tile, side), arrived.dtype),
            jax.ShapeDtypeStruct((1, side), jnp.int32),
        ),
        in_specs=[
            pl.BlockSpec(memory_space=pltpu.SMEM),
            pl.BlockSpec(memory_space=pltpu.VMEM),
        ],
        out_specs=(pl.BlockSpec(memory_space=pltpu.VMEM), pl.BlockSpec(memory_space=pltpu.VMEM)),
        scratch_shapes=[
            pltpu.VMEM((2, side), jnp.int32),
            pltpu.SMEM((2, side), jnp.int32),
            pltpu.SemaphoreType.DMA,
        ],
        name="pick",
    )(wanted, arrived)


def transform_kernel(
    source_ref,
    key_ref,
    row_len_ref,
    col_len_ref,
    window_ref,
    incoming_ref,
    out_ref,
    slab_ref,
    left_ref,
    held_ref,
    slab_sem,
    left_sems,
    out_sems,
):
    keys, side, _ = slab_ref.shape
    count, pieces, _, tile, _ = left_ref.shape
    depth = held_ref.shape[0]

    def fetch_left(g):
        return pltpu.make_async_copy(
            window_ref.at[:, pl.ds(g * INTER, INTER)], left_ref.at[g], left_sems.at[g]
        )

    def store(g, slot):
        return pltpu.make_async_copy(held_ref.at[slot], out_ref.at[g], out_sems.at[slot])

    def fetch(k, carry):
        pltpu.make_async_copy(incoming_ref.at[source_ref[0, k]], slab_ref.at[k], slab_sem).start()
        return carry

    def start_left(g, carry):
        fetch_left(g).start()
        return carry

    lax.fori_loop(0, keys, fetch, 0)
    lax.fori_loop(0, count, start_left, 0)
    pltpu.make_async_copy(incoming_ref.at[pl.ds(0, keys)], slab_ref, slab_sem).wait()

    def one_row(g, carry):
        slot = lax.rem(g, depth)
        row_len = row_len_ref[g]
        fetch_left(g).wait()

        @pl.when(g >= depth)
        def _():
            store(g - depth, slot).wait()

        def compute(height):
            lanes = lax.broadcasted_iota(jnp.int32, (height, side), 1)
            rows = lax.broadcasted_iota(jnp.int32, (height, side), 0)
            lefts = [left_ref[g, : height // tile, k].reshape(height, side) for k in range(INTER)]
            for y in range(YB):
                total = jnp.dot(
                    lefts[0], slab_ref[key_ref[g * INTER] + y], preferred_element_type=jnp.float32
                )
                for k in range(1, INTER):
                    total += jnp.dot(
                        lefts[k],
                        slab_ref[key_ref[g * INTER + k] + y],
                        preferred_element_type=jnp.float32,
                    )
                keep = (rows < row_len) & (lanes < col_len_ref[y])
                held_ref[slot, y, :height, :] = jnp.where(
                    keep, total * (1.0 / INTER), 0.0
                ).astype(held_ref.dtype)

        @pl.when(row_len > side // 2)
        def _():
            compute(side)

        @pl.when(row_len <= side // 2)
        def _():
            compute(side // 2)
            held_ref[slot, :, side // 2 :, :] = jnp.zeros((YB, side // 2, side), held_ref.dtype)

        store(g, slot).start()
        return carry

    lax.fori_loop(0, count, one_row, 0)
    for g in range(count - depth, count):
        store(g, g % depth).wait()


def transform(incoming, window, source, key, row_len, col_len):
    pieces, entries, tile, side = window.shape
    count = entries // INTER
    keys = NZ * YB
    anywhere = pl.BlockSpec(memory_space=pl.ANY)
    return pl.pallas_call(
        transform_kernel,
        out_shape=jax.ShapeDtypeStruct((row_len.shape[0], YB, side, side), incoming.dtype),
        in_specs=[pl.BlockSpec(memory_space=pltpu.SMEM)] * 4 + [anywhere] * 2,
        out_specs=anywhere,
        scratch_shapes=[
            pltpu.VMEM((keys, side, side), incoming.dtype),
            pltpu.VMEM((count, pieces, INTER, tile, side), incoming.dtype),
            pltpu.VMEM((STORES, YB, side, side), incoming.dtype),
            pltpu.SemaphoreType.DMA,
            pltpu.SemaphoreType.DMA((count,)),
            pltpu.SemaphoreType.DMA((STORES,)),
        ],
        cost_estimate=pl.CostEstimate(
            flops=2 * count * YB * INTER * side**3,
            bytes_accessed=2 * (keys + count * (YB + INTER)) * side * side,
            transcendentals=0,
        ),
        compiler_params=pltpu.CompilerParams(vmem_limit_bytes=TRANSFORM_VMEM),
        name="transform",
    )(source, key, row_len, col_len, window, incoming)


def shards(posteriors, pair_anchor, pair_column, inter, lengths):
    devices = lax.axis_size(AXES)
    pieces = lax.axis_size("row")
    owners = lax.axis_size("col")
    me = lax.axis_index(AXES)
    owner = lax.axis_index("col")
    slots, side, _ = posteriors.shape
    x_count = inter.shape[0]
    tile = side // pieces

    slot_target = pair_column // YB
    slot_key = pair_anchor * YB + pair_column % YB
    aims = slot_target[None, :] == jnp.arange(devices, dtype=jnp.int32)[:, None]
    sent_key = slots + jnp.sum(jnp.where(aims, slot_key[None, :] - slots, 0), axis=1)
    slot_ids = jnp.arange(slots, dtype=jnp.int32)
    owner_slot = jnp.sum(jnp.where(aims[:owners], slot_ids[None, :], 0), axis=1)

    cut = window_pieces(posteriors, owner_slot, sent_key, pieces)
    arrived = lax.all_to_all(
        cut.reshape(devices, tile + 8, side), AXES, split_axis=0, concat_axis=0, tiled=True
    )

    local_x = lax.dynamic_slice_in_dim(inter, owner * YB, YB, 0)
    window_keys = local_x * YB + jnp.arange(YB, dtype=jnp.int32)[:, None]
    picked, source = pick(arrived, window_keys.reshape(-1), tile)
    col_len = lax.dynamic_slice_in_dim(lengths, me * YB, YB, 0)
    row_len = lengths[:x_count]
    key = (inter * YB).reshape(-1)

    outgoing = pack(posteriors, slot_target, devices)
    outgoing, picked, source, col_len, row_len, key = lax.optimization_barrier(
        (outgoing, picked, source, col_len, row_len, key)
    )
    window = lax.all_gather(picked, AXES, axis=0, tiled=False)
    incoming = lax.all_to_all(outgoing, AXES, split_axis=0, concat_axis=0, tiled=True)
    window = window.reshape(pieces, x_count * INTER, tile, side)
    return transform(incoming, window, source, key, row_len, col_len)


def solution(mesh):
    return jax.shard_map(
        shards,
        mesh=mesh,
        in_specs=(P(AXES, None, None), P(AXES), P(AXES), P(), P()),
        out_specs=P(None, AXES, None, None),
        check_vma=False,
    )
```

time: 730 us -> 321 us (0.44)
  waiting for transfers between devices: 410 us -> 47.2 us
  blocking collectives: 0 us -> 201 us
  local copies, waits for them, and re-layouts: 177 us -> 3.82 us
  matrix products: 101 us -> 0 us
  Pallas kernels: 0 us -> 41.8 us
  starting transfers between devices: 21.7 us -> 11.7 us
    all_to_all x2 -> x1, waiting for transfers between devices: 225 us -> 14.8 us  [shards(): lax.all_to_all(cut.reshape(devices, tile + 8, side), AXES, split_axis=0,...]
    all_to_all x0 -> x1, blocking collectives: none -> 201 us  [shards(): lax.all_to_all(outgoing, AXES, split_axis=0, concat_axis=0, tiled=True)]
    psum x1 -> x0, waiting for transfers between devices: 185 us -> none  [broadcast(): return lax.psum(block, axis)]
    dot_general x4 -> x0, matrix products: 101 us -> none  [shards(): jnp.einsum('xmi,xymj->xyij', left_side, right_side, preferred_element_typ...]
    scatter x3 -> x0, local copies, waits for them, and re-layouts: 64.5 us -> none  [the longest x1 41.8 us: shards(): slab = jnp.zeros((NZ * col_block, side_len, side_len), jnp.bfloat16).at[i...]
    gather x5 -> x0, local copies, waits for them, and re-layouts: 47.5 us -> none  [the longest x4 43.4 us: shards(): right_side = slab[inter[:, term]]]
    pallas_call x0 -> x4, Pallas kernels: none -> 41.8 us  [the longest x1 25.6 us: transform(): pl.pallas_call(transform_kernel, out_shape=jax.ShapeDtypeStruct((row_len....]
    all_gather x0 -> x1, waiting for transfers between devices: none -> 32.4 us  [shards(): window = lax.all_gather(picked, AXES, axis=0, tiled=False)]
  transfers between devices with their start and end apart: 3 -> 2, of which waited for: 2 -> 2; matrix products, arithmetic and copies ran while one was open for 10% -> 1% of each run, Pallas kernels for 0% -> 2%
where the time goes in v1:
time: 321 us
  blocking collectives  201 us (63%)
  waiting for transfers between devices  47.2 us (15%)
  Pallas kernels  41.8 us (13%)
  between operations  13.5 us (4%)
  starting transfers between devices  11.7 us (4%)
  local copies, waits for them, and re-layouts  3.82 us (1%)
    all_to_all x1, blocking collectives, shards(): lax.all_to_all(outgoing, AXES, split_axis=0, concat_axis=0, tiled=True)  201 us
    all_gather x1, waiting for transfers between devices, shards(): window = lax.all_gather(picked, AXES, axis=0, tiled=False)  32.4 us
    pallas_call x1, Pallas kernels, transform(): pl.pallas_call(transform_kernel, out_shape=jax.ShapeDtypeStruct((row_len....  25.6 us
    all_to_all x1, waiting for transfers between devices, shards(): lax.all_to_all(cut.reshape(devices, tile + 8, side), AXES, split_axis=0,...  14.8 us
    all_to_all x1, starting transfers between devices, shards(): lax.all_to_all(cut.reshape(devices, tile + 8, side), AXES, split_axis=0,...  11.6 us
    pallas_call x1, Pallas kernels, pack(): pl.pallas_call(pack_kernel, out_shape=jax.ShapeDtypeStruct((devices, side...  6.98 us
  transfers between devices with their start and end apart: 2, of which 2 were waited for; matrix products, arithmetic and copies ran while one was open for 1% of the time, Pallas kernels for 2%

profile of v1, /device:TPU:1, one launch (start us, length us, event | category | flops | bytes accessed | tf_op | source)
XLA Modules:
  0.0 321.1 jit_solution(3032893116089243721)
XLA Ops:
  6.5 0.7 fusion.1
  7.2 0.0 copy-start.2
  7.2 0.1 iota_compare_fusion
  7.3 0.1 select_reduce_fusion
  7.4 0.6 broadcast_add_fusion.sent_key_ref
  8.0 0.5 select_reduce_fusion.1.owner_slot_ref
  8.5 0.0 copy-start.1
  8.5 0.0 copy-start.3
  8.5 6.1 %pieces.1 = bf16[16,8,24,256]{3,2,1,0:T(8,128)(2,1)} custom-call(s32[8]{0:T(128)} %select_reduce_fusion.1.owner_slot_ref, s32[128]{0:T(128)} %broadcast_add_fusion.sent_key_ref, bf16[64,256,256]{2,1,0:T(8,128)(2,1)} %block_ref.1), custom_call_target="tpu_custom_call" | custom-call | tf_op jit(solution)/shard_map/pieces/pallas_call | solution.py:75
  14.6 11.6 %all-to-all-start = ((bf16[128,24,256]{2,1,0:T(8,128)(2,1)}), bf16[128,24,256]{2,1,0:T(8,128)(2,1)S(1)}, u32[]{:S(2)}, u32[]{:S(2)}) async-start(bf16[128,24,256]{2,1,0:T(8,128)(2,1)} %bitcast.2), calls=%async_computation | async-start | bytes 3145728 | tf_op jit(solution)/shard_map/all_to_all | solution.py:258
  26.3 0.0 all-gather.3.cloned.1.call-start
  26.3 0.0 copy-done.2
  26.3 7.0 %pack.1 = bf16[128,256,256]{2,1,0:T(8,128)(2,1)} custom-call(s32[64]{0:T(128)} %copy-done.2, bf16[64,256,256]{2,1,0:T(8,128)(2,1)} %block_ref.1), custom_call_target="tpu_custom_call" | custom-call | tf_op jit(solution)/shard_map/pack/pallas_call | solution.py:40
  33.3 0.0 copy-done.1
  33.3 0.1 iota_add_fusion
  33.4 0.1 copy.12
  33.5 0.6 reshape.15.wanted_ref
  34.1 0.0 copy-done.3
  34.1 0.6 slice.7.row_len_ref
  34.7 0.7 dynamic_slice.7.col_len_ref
  35.4 0.1 copy.14
  35.5 0.6 reshape.17.key_ref
  36.1 14.8 %all-to-all-done.arrived_ref = bf16[128,24,256]{2,1,0:T(8,128)(2,1)S(1)} async-done(((bf16[128,24,256]{2,1,0:T(8,128)(2,1)}), bf16[128,24,256]{2,1,0:T(8,128)(2,1)S(1)}, u32[]{:S(2)}, u32[]{:S(2)}) %all-to-all-start) | async-done | bytes 1572896 | tf_op jit(solution)/shard_map/all_to_all | solution.py:258
  50.9 0.0 copy-start
  50.9 1.2 copy-done
  52.0 3.1 pick.1
  55.1 0.0 all-gather.3.cloned.1.call-update
  55.2 201.0 %all_to_all.10.incoming_ref = bf16[128,256,256]{2,1,0:T(8,128)(2,1)} all-to-all(bf16[128,256,256]{2,1,0:T(8,128)(2,1)} %pack.1), channel_id=1, replica_groups=mesh['row'=16,'col'=8] {'row','col'}, dimensions={0} | all-to-all | bytes 33554432 | tf_op jit(solution)/shard_map/all_to_all | solution.py:274
  256.2 32.4 %all-gather.3.cloned.1.call-done = bf16[2048,16,256]{2,1,0:T(8,128)(2,1)} async-done(((bf16[16,16,256]{2,1,0:T(8,128)(2,1)}), bf16[2048,16,256]{2,1,0:T(8,128)(2,1)}) %all-gather.3.cloned.1.call-update) | async-done | bytes 16777232 | tf_op jit(solution)/shard_map/all_gather | solution.py:273
  288.6 25.6 %transform.1 = bf16[32,4,256,256]{3,2,1,0:T(8,128)(2,1)} custom-call(s32[1,256]{1,0:T(1,128)} %get-tuple-element.15.source_ref, s32[128]{0:T(128)} %reshape.17.key_ref, s32[32]{0:T(128)} %slice.7.row_len_ref, s32[4]{0:T(128)} %dynamic_slice.7.col_len_ref, bf16[16,128,16,256]{3,2,1,0:T(8,128)(2,1)} %bitcast.3, bf16[128,256,256]{2,1,0:T(8,128)(2,1)} %all_to_all.10.incoming_ref), custom_call_target="tpu_custom_call" | custom-call | flops 17179869184 | bytes 41943040 | tf_op jit(solution)/shard_map/transform/pallas_call | solution.py:217
  (1 shorter events, 0.0 us)
Async XLA Ops:
  7.2 19.1 %copy-start.2 = (s32[64]{0:T(128)}, s32[64]{0:T(128)S(1)}, u32[]{:S(2)}) copy-start(s32[64]{0:T(128)S(1)} %get-tuple-element.22.slot_target_ref) | copy-start | bytes 772
  8.5 24.8 %copy-start.1 = (s32[32,4]{0,1:T(4,128)S(1)}, s32[32,4]{0,1:T(4,128)}, u32[]{:S(2)}) copy-start(s32[32,4]{0,1:T(4,128)} %param.8) | copy-start | bytes 1540
  8.5 25.6 %copy-start.3 = (s32[512]{0:T(512)S(1)}, s32[512]{0:T(512)}, u32[]{:S(2)}) copy-start(s32[512]{0:T(512)} %param.9) | copy-start | bytes 6148
  14.6 36.2 %all-to-all-start = ((bf16[128,24,256]{2,1,0:T(8,128)(2,1)}), bf16[128,24,256]{2,1,0:T(8,128)(2,1)S(1)}, u32[]{:S(2)}, u32[]{:S(2)}) async-start(bf16[128,24,256]{2,1,0:T(8,128)(2,1)} %bitcast.2), calls=%async_computation | async-start | bytes 3145728 | tf_op jit(solution)/shard_map/all_to_all | solution.py:258
  26.3 262.3 %all-gather.3.cloned.1.call-start = ((), (), s32[]{:S(2)}) async-start(), calls=%async_computation.2 | async-start | bytes 16908288 | tf_op jit(solution)/shard_map/all_gather | solution.py:273
  50.9 1.2 copy-start
Sparse Core Ops, SparseCore 0:
  55.3 233.2 all-gather.2

commit v2 on v1

--- a/solution.py
+++ b/solution.py
@@ -1,3 +1,5 @@
+import functools
+
 import jax
 import jax.numpy as jnp
 from jax import lax
@@ -11,7 +13,7 @@
 STORES = 4
 AXES = ("row", "col")
 VMEM_LIMIT = 56 * 1024 * 1024
-TRANSFORM_VMEM = 56 * 1024 * 1024
+SMALL_VMEM = 8 * 1024 * 1024
 
 
 def pack_kernel(slot_target_ref, blocks_ref, out_ref, held_ref, load_sems, store_sem):
@@ -55,43 +57,58 @@
     )(slot_target, posteriors)
 
 
-def pieces_kernel(owner_slot_ref, sent_key_ref, block_ref, out_ref):
-    pieces, _, rows, side = out_ref.shape
+def pieces_kernel(owner_slot_ref, sent_key_ref, blocks_ref, out_ref, held_ref, sems):
+    pieces, owners, rows, half = out_ref.shape
+    side = 2 * half
     tile = side // pieces
-    o = pl.program_id(0)
-    owners = pl.num_programs(0)
-    turned = block_ref[0].T
-    out_ref[:, 0, :tile, :] = turned.reshape(pieces, tile, side)
-    for p in range(pieces):
-        first = lax.broadcasted_iota(jnp.int32, (rows - tile, side), 0) < (rows - tile) // 2
-        keys = jnp.where(first, sent_key_ref[p * owners + o], sent_key_ref[o])
-        out_ref[p, 0, tile:, :] = keys.astype(jnp.float32).astype(out_ref.dtype)
+    header = 2 * tile
+
+    def load(o):
+        return pltpu.make_async_copy(
+            blocks_ref.at[owner_slot_ref[o]], held_ref.at[o], sems.at[o]
+        )
+
+    for o in range(owners):
+        load(o).start()
+    first = lax.broadcasted_iota(jnp.int32, (rows - header, half), 0) < (rows - header) // 2
+    for o in range(owners):
+        for p in range(pieces):
+            keys = jnp.where(first, sent_key_ref[p * owners + o], sent_key_ref[o])
+            out_ref[p, o, header:, :] = keys.astype(jnp.float32).astype(out_ref.dtype)
+    for o in range(owners):
+        load(o).wait()
+        turned = held_ref[o].T
+        for part in range(2):
+            out_ref[:, o, part * tile : (part + 1) * tile, :] = turned[
+                :, part * half : (part + 1) * half
+            ].reshape(pieces, tile, half)
 
 
 def window_pieces(posteriors, owner_slot, sent_key, pieces):
     _, side, _ = posteriors.shape
     owners = owner_slot.shape[0]
-    rows = side // pieces + 8
+    rows = 2 * side // pieces + 8
     return pl.pallas_call(
         pieces_kernel,
-        out_shape=jax.ShapeDtypeStruct((pieces, owners, rows, side), posteriors.dtype),
-        grid_spec=pltpu.PrefetchScalarGridSpec(
-            num_scalar_prefetch=2,
-            grid=(owners,),
-            in_specs=[pl.BlockSpec((1, side, side), lambda o, slot, key: (slot[o], 0, 0))],
-            out_specs=pl.BlockSpec((pieces, 1, rows, side), lambda o, slot, key: (0, o, 0, 0)),
-        ),
+        out_shape=jax.ShapeDtypeStruct((pieces, owners, rows, side // 2), posteriors.dtype),
+        in_specs=[pl.BlockSpec(memory_space=pltpu.SMEM)] * 2 + [pl.BlockSpec(memory_space=pl.ANY)],
+        out_specs=pl.BlockSpec(memory_space=pltpu.VMEM),
+        scratch_shapes=[
+            pltpu.VMEM((owners, side, side), posteriors.dtype),
+            pltpu.SemaphoreType.DMA((owners,)),
+        ],
+        compiler_params=pltpu.CompilerParams(vmem_limit_bytes=VMEM_LIMIT),
         name="pieces",
     )(owner_slot, sent_key, posteriors)
 
 
 def pick_kernel(wanted_ref, arrived_ref, picked_ref, source_ref, found_ref, where_ref, sem):
     wanted, tile, side = picked_ref.shape
-    devices = arrived_ref.shape[0]
-    keys = lax.broadcasted_iota(jnp.int32, (devices, side), 1)
-    device = lax.broadcasted_iota(jnp.int32, (devices, side), 0)
+    devices, _, half = arrived_ref.shape
+    keys = lax.broadcasted_iota(jnp.int32, (devices, half), 1)
+    device = lax.broadcasted_iota(jnp.int32, (devices, half), 0)
     for part in range(2):
-        got = arrived_ref[:, tile + 4 * part, :].astype(jnp.float32).astype(jnp.int32)
+        got = arrived_ref[:, 2 * tile + 4 * part, :].astype(jnp.float32).astype(jnp.int32)
         found = jnp.sum(jnp.where(got == keys, device, 0), axis=0, keepdims=True)
         found_ref[pl.ds(part, 1), :] = found
     source_ref[...] = found_ref[pl.ds(0, 1), :]
@@ -99,17 +116,19 @@
     copy.start()
     copy.wait()
     for q in range(wanted):
-        picked_ref[q] = arrived_ref[where_ref[1, wanted_ref[q]], :tile, :]
+        sender = where_ref[1, wanted_ref[q]]
+        picked_ref[q, :, :half] = arrived_ref[sender, :tile, :]
+        picked_ref[q, :, half:] = arrived_ref[sender, tile : 2 * tile, :]
 
 
 def pick(arrived, wanted, tile):
-    devices, _, side = arrived.shape
+    half = arrived.shape[2]
     count = wanted.shape[0]
     return pl.pallas_call(
         pick_kernel,
         out_shape=(
-            jax.ShapeDtypeStruct((count, tile, side), arrived.dtype),
-            jax.ShapeDtypeStruct((1, side), jnp.int32),
+            jax.ShapeDtypeStruct((count, tile, 2 * half), arrived.dtype),
+            jax.ShapeDtypeStruct((1, half), jnp.int32),
         ),
         in_specs=[
             pl.BlockSpec(memory_space=pltpu.SMEM),
@@ -117,10 +136,11 @@
         ],
         out_specs=(pl.BlockSpec(memory_space=pltpu.VMEM), pl.BlockSpec(memory_space=pltpu.VMEM)),
         scratch_shapes=[
-            pltpu.VMEM((2, side), jnp.int32),
-            pltpu.SMEM((2, side), jnp.int32),
+            pltpu.VMEM((2, half), jnp.int32),
+            pltpu.SMEM((2, half), jnp.int32),
             pltpu.SemaphoreType.DMA,
         ],
+        compiler_params=pltpu.CompilerParams(vmem_limit_bytes=SMALL_VMEM),
         name="pick",
     )(wanted, arrived)
 
@@ -136,7 +156,7 @@
     slab_ref,
     left_ref,
     held_ref,
-    slab_sem,
+    slab_sems,
     left_sems,
     out_sems,
 ):
@@ -152,22 +172,43 @@
     def store(g, slot):
         return pltpu.make_async_copy(held_ref.at[slot], out_ref.at[g], out_sems.at[slot])
 
-    def fetch(k, carry):
-        pltpu.make_async_copy(incoming_ref.at[source_ref[0, k]], slab_ref.at[k], slab_sem).start()
+    def fetch(k, sem):
+        pltpu.make_async_copy(incoming_ref.at[source_ref[0, k]], slab_ref.at[k], sem).start()
+
+    def wait_blocks(amount, sem):
+        part = pl.ds(0, amount)
+        pltpu.make_async_copy(incoming_ref.at[part], slab_ref.at[part], sem).wait()
+
+    def fetch_other(anchor, carry):
+        used = [key_ref[k] == anchor * YB for k in range(INTER)]
+
+        @pl.when(~functools.reduce(jnp.logical_or, used))
+        def _():
+            for y in range(YB):
+                fetch(anchor * YB + y, slab_sems.at[1])
+
         return carry
 
     def start_left(g, carry):
         fetch_left(g).start()
         return carry
 
-    lax.fori_loop(0, keys, fetch, 0)
-    lax.fori_loop(0, count, start_left, 0)
-    pltpu.make_async_copy(incoming_ref.at[pl.ds(0, keys)], slab_ref, slab_sem).wait()
+    fetch_left(0).start()
+    for k in range(INTER):
+        for y in range(YB):
+            fetch(key_ref[k] + y, slab_sems.at[0])
+    lax.fori_loop(0, keys // YB, fetch_other, 0)
+    lax.fori_loop(1, count, start_left, 0)
+    wait_blocks(INTER * YB, slab_sems.at[0])
 
     def one_row(g, carry):
         slot = lax.rem(g, depth)
         row_len = row_len_ref[g]
         fetch_left(g).wait()
+
+        @pl.when(g == 1)
+        def _():
+            wait_blocks(keys - INTER * YB, slab_sems.at[1])
 
         @pl.when(g >= depth)
         def _():
@@ -223,7 +264,7 @@
             pltpu.VMEM((keys, side, side), incoming.dtype),
             pltpu.VMEM((count, pieces, INTER, tile, side), incoming.dtype),
             pltpu.VMEM((STORES, YB, side, side), incoming.dtype),
-            pltpu.SemaphoreType.DMA,
+            pltpu.SemaphoreType.DMA((2,)),
             pltpu.SemaphoreType.DMA((count,)),
             pltpu.SemaphoreType.DMA((STORES,)),
         ],
@@ -232,7 +273,7 @@
             bytes_accessed=2 * (keys + count * (YB + INTER)) * side * side,
             transcendentals=0,
         ),
-        compiler_params=pltpu.CompilerParams(vmem_limit_bytes=TRANSFORM_VMEM),
+        compiler_params=pltpu.CompilerParams(vmem_limit_bytes=VMEM_LIMIT),
         name="transform",
     )(source, key, row_len, col_len, window, incoming)
 
@@ -256,7 +297,7 @@
 
     cut = window_pieces(posteriors, owner_slot, sent_key, pieces)
     arrived = lax.all_to_all(
-        cut.reshape(devices, tile + 8, side), AXES, split_axis=0, concat_axis=0, tiled=True
+        cut.reshape(devices, 2 * tile + 8, side // 2), AXES, split_axis=0, concat_axis=0, tiled=True
     )
 
     local_x = lax.dynamic_slice_in_dim(inter, owner * YB, YB, 0)

time: 321 us -> 313 us (0.975)
  Pallas kernels: 41.8 us -> 36.9 us
where the time goes in v2:
time: 313 us; the launch traced here: 312 us
  blocking collectives  201 us (64%)
  waiting for transfers between devices  44.9 us (14%)
  Pallas kernels  36.9 us (12%)
  between operations  13.5 us (4%)
  starting transfers between devices  11.5 us (4%)
    all_to_all x1, blocking collectives, shards(): lax.all_to_all(outgoing, AXES, split_axis=0, concat_axis=0, tiled=True)  201 us
    all_gather x1, waiting for transfers between devices, shards(): window = lax.all_gather(picked, AXES, axis=0, tiled=False)  32.3 us
    pallas_call x1, Pallas kernels, transform(): pl.pallas_call(transform_kernel, out_shape=jax.ShapeDtypeStruct((row_len....  24.4 us
    all_to_all x1, waiting for transfers between devices, shards(): lax.all_to_all(cut.reshape(devices, 2 * tile + 8, side // 2), AXES, split...  12.6 us
    all_to_all x1, starting transfers between devices, shards(): lax.all_to_all(cut.reshape(devices, 2 * tile + 8, side // 2), AXES, split...  11.5 us
    pallas_call x1, Pallas kernels, pack(): pl.pallas_call(pack_kernel, out_shape=jax.ShapeDtypeStruct((devices, side...  6.98 us
  transfers between devices with their start and end apart: 2, of which 2 were waited for; matrix products, arithmetic and copies ran while one was open for 1% of the time, Pallas kernels for 2%

profile of v2, /device:TPU:1, one launch (start us, length us, event | category | flops | bytes accessed | tf_op | source)
XLA Modules:
  0.0 312.4 jit_solution(17475284841140953232)
XLA Ops:
  6.5 0.7 fusion.1
  7.2 0.0 copy-start.2
  7.2 0.1 iota_compare_fusion
  7.3 0.1 select_reduce_fusion
  7.4 0.6 broadcast_add_fusion.sent_key_ref
  8.0 0.5 select_reduce_fusion.1.owner_slot_ref
  8.5 0.0 copy-start.1
  8.5 0.0 copy-start.3
  8.5 3.6 %pieces.1 = bf16[16,8,40,128]{3,2,1,0:T(8,128)(2,1)} custom-call(s32[8]{0:T(128)} %select_reduce_fusion.1.owner_slot_ref, s32[128]{0:T(128)} %broadcast_add_fusion.sent_key_ref, bf16[64,256,256]{2,1,0:T(8,128)(2,1)} %blocks_ref.3), custom_call_target="tpu_custom_call" | custom-call | tf_op jit(solution)/shard_map/pieces/pallas_call | solution.py:91
  12.1 11.5 %all-to-all-start = ((bf16[128,40,128]{2,1,0:T(8,128)(2,1)}), bf16[128,40,128]{2,1,0:T(8,128)(2,1)S(1)}, u32[]{:S(2)}, u32[]{:S(2)}) async-start(bf16[128,40,128]{2,1,0:T(8,128)(2,1)} %bitcast.2), calls=%async_computation | async-start | bytes 2621440 | tf_op jit(solution)/shard_map/all_to_all | solution.py:299
  23.6 0.0 all-gather.3.cloned.1.call-start
  23.6 0.0 copy-done.2
  23.7 7.0 %pack.1 = bf16[128,256,256]{2,1,0:T(8,128)(2,1)} custom-call(s32[64]{0:T(128)} %copy-done.2, bf16[64,256,256]{2,1,0:T(8,128)(2,1)} %blocks_ref.3), custom_call_target="tpu_custom_call" | custom-call | tf_op jit(solution)/shard_map/pack/pallas_call | solution.py:42
  30.7 0.0 copy-done.1
  30.7 0.1 iota_add_fusion
  30.7 0.1 copy.12
  30.8 0.1 reshape.15.wanted_ref
  30.9 0.0 copy-done.3
  30.9 0.5 slice.7.row_len_ref
  31.4 0.6 dynamic_slice.7.col_len_ref
  32.1 0.1 copy.14
  32.2 0.6 reshape.17.key_ref
  32.8 12.6 %all-to-all-done.arrived_ref = bf16[128,40,128]{2,1,0:T(8,128)(2,1)S(1)} async-done(((bf16[128,40,128]{2,1,0:T(8,128)(2,1)}), bf16[128,40,128]{2,1,0:T(8,128)(2,1)S(1)}, u32[]{:S(2)}, u32[]{:S(2)}) %all-to-all-start) | async-done | bytes 1310752 | tf_op jit(solution)/shard_map/all_to_all | solution.py:299
  45.4 2.0 pick.1
  47.4 0.0 copy-start
  47.4 0.6 copy-done
  48.0 0.0 all-gather.3.cloned.1.call-update
  48.0 200.9 %all_to_all.10.incoming_ref = bf16[128,256,256]{2,1,0:T(8,128)(2,1)} all-to-all(bf16[128,256,256]{2,1,0:T(8,128)(2,1)} %pack.1), channel_id=1, replica_groups=mesh['row'=16,'col'=8] {'row','col'}, dimensions={0} | all-to-all | bytes 33554432 | tf_op jit(solution)/shard_map/all_to_all | solution.py:315
  248.9 32.3 %all-gather.3.cloned.1.call-done = bf16[2048,16,256]{2,1,0:T(8,128)(2,1)} async-done(((bf16[16,16,256]{2,1,0:T(8,128)(2,1)}), bf16[2048,16,256]{2,1,0:T(8,128)(2,1)}) %all-gather.3.cloned.1.call-update) | async-done | bytes 16777232 | tf_op jit(solution)/shard_map/all_gather | solution.py:314
  281.2 24.4 %transform.1 = bf16[32,4,256,256]{3,2,1,0:T(8,128)(2,1)} custom-call(s32[1,128]{1,0:T(1,128)} %copy-done, s32[128]{0:T(128)} %reshape.17.key_ref, s32[32]{0:T(128)} %slice.7.row_len_ref, s32[4]{0:T(128)} %dynamic_slice.7.col_len_ref, bf16[16,128,16,256]{3,2,1,0:T(8,128)(2,1)} %bitcast.3, bf16[128,256,256]{2,1,0:T(8,128)(2,1)} %all_to_all.10.incoming_ref), custom_call_target="tpu_custom_call" | custom-call | flops 17179869184 | bytes 41943040 | tf_op jit(solution)/shard_map/transform/pallas_call | solution.py:258
  (1 shorter events, 0.0 us)
Async XLA Ops:
  7.2 16.4 %copy-start.2 = (s32[64]{0:T(128)}, s32[64]{0:T(128)S(1)}, u32[]{:S(2)}) copy-start(s32[64]{0:T(128)S(1)} %get-tuple-element.22.slot_target_ref) | copy-start | bytes 772
  8.5 22.1 %copy-start.1 = (s32[32,4]{0,1:T(4,128)S(1)}, s32[32,4]{0,1:T(4,128)}, u32[]{:S(2)}) copy-start(s32[32,4]{0,1:T(4,128)} %param.8) | copy-start | bytes 1540
  8.5 22.4 %copy-start.3 = (s32[512]{0:T(512)S(1)}, s32[512]{0:T(512)}, u32[]{:S(2)}) copy-start(s32[512]{0:T(512)} %param.9) | copy-start | bytes 6148
  12.1 33.3 %all-to-all-start = ((bf16[128,40,128]{2,1,0:T(8,128)(2,1)}), bf16[128,40,128]{2,1,0:T(8,128)(2,1)S(1)}, u32[]{:S(2)}, u32[]{:S(2)}) async-start(bf16[128,40,128]{2,1,0:T(8,128)(2,1)} %bitcast.2), calls=%async_computation | async-start | bytes 2621440 | tf_op jit(solution)/shard_map/all_to_all | solution.py:299
  23.6 257.6 %all-gather.3.cloned.1.call-start = ((), (), s32[]{:S(2)}) async-start(), calls=%async_computation.2 | async-start | bytes 16908288 | tf_op jit(solution)/shard_map/all_gather | solution.py:314
  47.4 0.6 copy-start
Sparse Core Ops, SparseCore 0:
  48.1 233.0 all-gather.2

commit v3 on v2

--- a/solution.py
+++ b/solution.py
@@ -16,7 +16,7 @@
 SMALL_VMEM = 8 * 1024 * 1024
 
 
-def pack_kernel(slot_target_ref, blocks_ref, out_ref, held_ref, load_sems, store_sem):
+def pack_kernel(column_ref, blocks_ref, out_ref, held_ref, load_sems, store_sem):
     chunks = load_sems.shape[0]
     slots = held_ref.shape[0]
     chunk = slots // chunks
@@ -31,12 +31,12 @@
         load(c).wait()
         for s in range(c * chunk, (c + 1) * chunk):
             pltpu.make_async_copy(
-                held_ref.at[s], out_ref.at[slot_target_ref[s]], store_sem
+                held_ref.at[s], out_ref.at[lax.div(column_ref[s], YB)], store_sem
             ).start()
     pltpu.make_async_copy(held_ref, out_ref.at[pl.ds(0, slots)], store_sem).wait()
 
 
-def pack(posteriors, slot_target, devices):
+def pack(posteriors, pair_column, devices):
     slots, side, _ = posteriors.shape
     chunks = 8
     return pl.pallas_call(
@@ -54,10 +54,12 @@
         ],
         compiler_params=pltpu.CompilerParams(vmem_limit_bytes=VMEM_LIMIT),
         name="pack",
-    )(slot_target, posteriors)
-
-
-def pieces_kernel(owner_slot_ref, sent_key_ref, blocks_ref, out_ref, held_ref, sems):
+    )(pair_column, posteriors)
+
+
+def pieces_kernel(
+    anchor_ref, column_ref, blocks_ref, out_ref, slot_ref, sent_key_ref, held_ref, sems
+):
     pieces, owners, rows, half = out_ref.shape
     side = 2 * half
     tile = side // pieces
@@ -65,9 +67,24 @@
 
     def load(o):
         return pltpu.make_async_copy(
-            blocks_ref.at[owner_slot_ref[o]], held_ref.at[o], sems.at[o]
+            blocks_ref.at[slot_ref[o]], held_ref.at[o], sems.at[o]
         )
 
+    slots = anchor_ref.shape[0]
+
+    def clear(d, carry):
+        slot_ref[d] = 0
+        sent_key_ref[d] = slots
+        return carry
+
+    def note(s, carry):
+        target = lax.div(column_ref[s], YB)
+        slot_ref[target] = s
+        sent_key_ref[target] = anchor_ref[s] * YB + lax.rem(column_ref[s], YB)
+        return carry
+
+    lax.fori_loop(0, pieces * owners, clear, 0, unroll=8)
+    lax.fori_loop(0, slots, note, 0, unroll=8)
     for o in range(owners):
         load(o).start()
     first = lax.broadcasted_iota(jnp.int32, (rows - header, half), 0) < (rows - header) // 2
@@ -84,9 +101,8 @@
             ].reshape(pieces, tile, half)
 
 
-def window_pieces(posteriors, owner_slot, sent_key, pieces):
+def window_pieces(posteriors, pair_anchor, pair_column, pieces, owners):
     _, side, _ = posteriors.shape
-    owners = owner_slot.shape[0]
     rows = 2 * side // pieces + 8
     return pl.pallas_call(
         pieces_kernel,
@@ -94,12 +110,14 @@
         in_specs=[pl.BlockSpec(memory_space=pltpu.SMEM)] * 2 + [pl.BlockSpec(memory_space=pl.ANY)],
         out_specs=pl.BlockSpec(memory_space=pltpu.VMEM),
         scratch_shapes=[
+            pltpu.SMEM((pieces * owners,), jnp.int32),
+            pltpu.SMEM((pieces * owners,), jnp.int32),
             pltpu.VMEM((owners, side, side), posteriors.dtype),
             pltpu.SemaphoreType.DMA((owners,)),
         ],
         compiler_params=pltpu.CompilerParams(vmem_limit_bytes=VMEM_LIMIT),
         name="pieces",
-    )(owner_slot, sent_key, posteriors)
+    )(pair_anchor, pair_column, posteriors)
 
 
 def pick_kernel(wanted_ref, arrived_ref, picked_ref, source_ref, found_ref, where_ref, sem):
@@ -284,18 +302,11 @@
     owners = lax.axis_size("col")
     me = lax.axis_index(AXES)
     owner = lax.axis_index("col")
-    slots, side, _ = posteriors.shape
+    side = posteriors.shape[1]
     x_count = inter.shape[0]
     tile = side // pieces
 
-    slot_target = pair_column // YB
-    slot_key = pair_anchor * YB + pair_column % YB
-    aims = slot_target[None, :] == jnp.arange(devices, dtype=jnp.int32)[:, None]
-    sent_key = slots + jnp.sum(jnp.where(aims, slot_key[None, :] - slots, 0), axis=1)
-    slot_ids = jnp.arange(slots, dtype=jnp.int32)
-    owner_slot = jnp.sum(jnp.where(aims[:owners], slot_ids[None, :], 0), axis=1)
-
-    cut = window_pieces(posteriors, owner_slot, sent_key, pieces)
+    cut = window_pieces(posteriors, pair_anchor, pair_column, pieces, owners)
     arrived = lax.all_to_all(
         cut.reshape(devices, 2 * tile + 8, side // 2), AXES, split_axis=0, concat_axis=0, tiled=True
     )
@@ -307,7 +318,7 @@
     row_len = lengths[:x_count]
     key = (inter * YB).reshape(-1)
 
-    outgoing = pack(posteriors, slot_target, devices)
+    outgoing = pack(posteriors, pair_column, devices)
     outgoing, picked, source, col_len, row_len, key = lax.optimization_barrier(
         (outgoing, picked, source, col_len, row_len, key)
     )

time: 313 us -> 312 us (level)
  no operation moved by 1% of the time
where the time goes in v3:
time: 312 us
  blocking collectives  201 us (64%)
  waiting for transfers between devices  44.5 us (14%)
  Pallas kernels  38.9 us (12%)
  between operations  13.5 us (4%)
  starting transfers between devices  11.6 us (4%)
    all_to_all x1, blocking collectives, shards(): lax.all_to_all(outgoing, AXES, split_axis=0, concat_axis=0, tiled=True)  201 us
    all_gather x1, waiting for transfers between devices, shards(): window = lax.all_gather(picked, AXES, axis=0, tiled=False)  32.1 us
    pallas_call x1, Pallas kernels, transform(): pl.pallas_call(transform_kernel, out_shape=jax.ShapeDtypeStruct((row_len....  25.7 us
    all_to_all x1, waiting for transfers between devices, shards(): lax.all_to_all(cut.reshape(devices, 2 * tile + 8, side // 2), AXES, split...  12.4 us
    all_to_all x1, starting transfers between devices, shards(): lax.all_to_all(cut.reshape(devices, 2 * tile + 8, side // 2), AXES, split...  11.5 us
    pallas_call x1, Pallas kernels, pack(): pl.pallas_call(pack_kernel, out_shape=jax.ShapeDtypeStruct((devices, side...  6.99 us
  transfers between devices with their start and end apart: 2, of which 2 were waited for; matrix products, arithmetic and copies ran while one was open for 1% of the time, Pallas kernels for 2%

profile of v3, /device:TPU:1, one launch (start us, length us, event | category | flops | bytes accessed | tf_op | source)
XLA Modules:
  0.0 312.3 jit_solution(7237655702161612692)
XLA Ops:
  6.5 0.0 copy-start.2
  6.5 0.0 copy-start.1
  6.5 4.2 %pieces.1 = bf16[16,8,40,128]{3,2,1,0:T(8,128)(2,1)} custom-call(s32[64]{0:T(128)} %anchor_ref.1, s32[64]{0:T(128)} %column_ref.3, bf16[64,256,256]{2,1,0:T(8,128)(2,1)} %blocks_ref.3), custom_call_target="tpu_custom_call" | custom-call | tf_op jit(solution)/shard_map/pieces/pallas_call | solution.py:107
  10.7 11.5 %all-to-all-start = ((bf16[128,40,128]{2,1,0:T(8,128)(2,1)}), bf16[128,40,128]{2,1,0:T(8,128)(2,1)S(1)}, u32[]{:S(2)}, u32[]{:S(2)}) async-start(bf16[128,40,128]{2,1,0:T(8,128)(2,1)} %bitcast.2), calls=%async_computation | async-start | bytes 2621440 | tf_op jit(solution)/shard_map/all_to_all | solution.py:310
  22.3 0.0 all-gather.3.cloned.1.call-start
  22.3 7.0 %pack.1 = bf16[128,256,256]{2,1,0:T(8,128)(2,1)} custom-call(s32[64]{0:T(128)} %column_ref.3, bf16[64,256,256]{2,1,0:T(8,128)(2,1)} %blocks_ref.3), custom_call_target="tpu_custom_call" | custom-call | tf_op jit(solution)/shard_map/pack/pallas_call | solution.py:42
  29.3 0.0 copy-done.2
  29.3 0.6 slice.3.row_len_ref
  29.9 0.7 dynamic_slice.7.col_len_ref
  30.6 0.0 copy-done.1
  30.6 0.1 iota_add_fusion
  30.6 0.1 copy.10
  30.7 0.1 reshape.12.wanted_ref
  30.8 0.1 copy.11
  30.9 0.7 reshape.14.key_ref
  31.6 12.4 %all-to-all-done.arrived_ref = bf16[128,40,128]{2,1,0:T(8,128)(2,1)S(1)} async-done(((bf16[128,40,128]{2,1,0:T(8,128)(2,1)}), bf16[128,40,128]{2,1,0:T(8,128)(2,1)S(1)}, u32[]{:S(2)}, u32[]{:S(2)}) %all-to-all-start) | async-done | bytes 1310752 | tf_op jit(solution)/shard_map/all_to_all | solution.py:310
  44.0 2.0 pick.1
  46.1 0.0 copy-start
  46.1 0.5 copy-done
  46.6 0.0 all-gather.3.cloned.1.call-update
  46.6 201.0 %all_to_all.10.incoming_ref = bf16[128,256,256]{2,1,0:T(8,128)(2,1)} all-to-all(bf16[128,256,256]{2,1,0:T(8,128)(2,1)} %pack.1), channel_id=1, replica_groups=mesh['row'=16,'col'=8] {'row','col'}, dimensions={0} | all-to-all | bytes 33554432 | tf_op jit(solution)/shard_map/all_to_all | solution.py:326
  247.6 32.1 %all-gather.3.cloned.1.call-done = bf16[2048,16,256]{2,1,0:T(8,128)(2,1)} async-done(((bf16[16,16,256]{2,1,0:T(8,128)(2,1)}), bf16[2048,16,256]{2,1,0:T(8,128)(2,1)}) %all-gather.3.cloned.1.call-update) | async-done | bytes 16777232 | tf_op jit(solution)/shard_map/all_gather | solution.py:325
  279.7 25.7 %transform.1 = bf16[32,4,256,256]{3,2,1,0:T(8,128)(2,1)} custom-call(s32[1,128]{1,0:T(1,128)} %copy-done, s32[128]{0:T(128)} %reshape.14.key_ref, s32[32]{0:T(128)} %slice.3.row_len_ref, s32[4]{0:T(128)} %dynamic_slice.7.col_len_ref, bf16[16,128,16,256]{3,2,1,0:T(8,128)(2,1)} %bitcast.3, bf16[128,256,256]{2,1,0:T(8,128)(2,1)} %all_to_all.10.incoming_ref), custom_call_target="tpu_custom_call" | custom-call | flops 17179869184 | bytes 41943040 | tf_op jit(solution)/shard_map/transform/pallas_call | solution.py:276
  (1 shorter events, 0.0 us)
Async XLA Ops:
  6.5 22.8 %copy-start.2 = (s32[512]{0:T(512)S(1)}, s32[512]{0:T(512)}, u32[]{:S(2)}) copy-start(s32[512]{0:T(512)} %param.9) | copy-start | bytes 6148
  6.5 24.0 %copy-start.1 = (s32[32,4]{0,1:T(4,128)S(1)}, s32[32,4]{0,1:T(4,128)}, u32[]{:S(2)}) copy-start(s32[32,4]{0,1:T(4,128)} %param.8) | copy-start | bytes 1540
  10.7 33.3 %all-to-all-start = ((bf16[128,40,128]{2,1,0:T(8,128)(2,1)}), bf16[128,40,128]{2,1,0:T(8,128)(2,1)S(1)}, u32[]{:S(2)}, u32[]{:S(2)}) async-start(bf16[128,40,128]{2,1,0:T(8,128)(2,1)} %bitcast.2), calls=%async_computation | async-start | bytes 2621440 | tf_op jit(solution)/shard_map/all_to_all | solution.py:310
  22.3 257.5 %all-gather.3.cloned.1.call-start = ((), (), s32[]{:S(2)}) async-start(), calls=%async_computation.2 | async-start | bytes 16908288 | tf_op jit(solution)/shard_map/all_gather | solution.py:325
  46.1 0.5 copy-start
Sparse Core Ops, SparseCore 0:
  46.7 232.9 all-gather.2
